TPU v7x, 32 devices: a whole 2x2x4 slice. The times are simulated.
32 devices in a mesh: expert: 8 (over z, y), replica: 4 (over x, core).
Axes of the slice: x: 2, y: 2, z: 4, core: 2. Of those that a mesh axis runs over, the one named last changes fastest.
Arguments:
- tokens: bfloat16 [4096, 2048], P(('expert', 'replica')), may hold values from -6 to 6
- out_grad: bfloat16 [4096, 2048], P(('expert', 'replica')), may hold values from -6 to 6
- expert_ids: int32 [4096, 2], P(('expert', 'replica')), may hold values from 0 to 3, as said below
- route_weights: bfloat16 [4096, 2], P(('expert', 'replica')), may hold values from 0.25 to 1
- capacity: int32 [4], replicated, may hold values from 2 to 2
- w_gate: bfloat16 [8, 2048, 384], P('expert', 'replica'), may hold values from -0.125 to 0.125
- w_up: bfloat16 [8, 2048, 384], P('expert', 'replica'), may hold values from -0.125 to 0.125
- w_down: bfloat16 [8, 384, 2048], P('expert', None, 'replica'), may hold values from -0.21875 to 0.21875
Outputs:
- x_grad: bfloat16 [4096, 2048], P(('expert', 'replica'))
- gate_grad: bfloat16 [8, 2048, 384], P('expert', 'replica')
- up_grad: bfloat16 [8, 2048, 384], P('expert', 'replica')
- down_grad: bfloat16 [8, 384, 2048], P('expert')
Inputs may be any that keep to these rules, and one draw needn't show every extreme that they name: `expert_ids`: each row names 2 different experts.
All inputs are finite; a program needn't handle non-finite values.
Results may differ from a plain program's by a relative error of at most 0.009.
Values may be sent and summed in bfloat16 or wider, within the bound.
A program may use at most 64 MiB of HBM per device.

v0:
```python
import jax
import jax.numpy as jnp
from jax import lax
from jax.sharding import PartitionSpec as P

CAP = 2


def shards(tokens, out_grad, expert_ids, route_weights, capacity, w_gate, w_up, w_down):
    experts = capacity.shape[0]
    owners = lax.axis_size("expert")
    width = tokens.shape[1]
    slot_count = experts * CAP
    expert_range = jnp.arange(experts, dtype=jnp.int32)
    chosen = (expert_ids[:, :, None] == expert_range[None, None, :]).astype(jnp.int32)
    ranks = jnp.cumsum(jnp.sum(chosen, axis=1), axis=0)
    place = jnp.sum(chosen * ranks[:, None, :], axis=2) - 1
    limit = jnp.sum(chosen * capacity[None, None, :], axis=2)
    slot_ids = jnp.where(place < limit, expert_ids * CAP + place, -1)
    table = slot_ids[None, :, :] == jnp.arange(slot_count, dtype=jnp.int32)[:, None, None]
    picker = jnp.any(table, axis=2).astype(jnp.bfloat16)
    slot_weight = jnp.sum(
        jnp.where(table, route_weights.astype(jnp.float32)[None, :, :], 0.0), axis=(1, 2)
    ).astype(jnp.bfloat16)
    packed = jnp.dot(
        picker, jnp.concatenate([tokens, out_grad], axis=1), preferred_element_type=jnp.float32
    ).astype(jnp.bfloat16)
    packed = packed.reshape(experts, CAP, 2 * width)
    slot_weight = slot_weight.reshape(experts, CAP)
    send_rows = jnp.broadcast_to(packed[:, None], (experts, 2, CAP, 2 * width)).reshape(
        owners, CAP, 2 * width
    )
    send_weight = jnp.broadcast_to(slot_weight[:, None], (experts, 2, CAP)).reshape(owners, CAP)
    got_rows, got_weight = (
        lax.all_to_all(send_rows, "expert", split_axis=0, concat_axis=0, tiled=True),
        lax.all_to_all(send_weight, "expert", split_axis=0, concat_axis=0, tiled=True),
    )
    gate_all, up_all, down_all = (
        lax.all_gather(w_gate, "replica", axis=1, tiled=True),
        lax.all_gather(w_up, "replica", axis=1, tiled=True),
        lax.all_gather(w_down, "replica", axis=2, tiled=True),
    )
    gate_mat = gate_all[0]
    up_mat = up_all[0]
    down_mat = down_all[0]
    row_total = owners * CAP
    flat_rows = got_rows.reshape(row_total, 2 * width)
    inputs = flat_rows[:, :width]
    cotangent = flat_rows[:, width:]
    weights = got_weight.reshape(row_total).astype(jnp.float32)
    gate = jnp.dot(inputs, gate_mat, preferred_element_type=jnp.float32)
    up = jnp.dot(inputs, up_mat, preferred_element_type=jnp.float32)
    sig = jax.nn.sigmoid(gate)
    act = gate * sig
    hidden = (act * up).astype(jnp.bfloat16)
    scaled = (weights[:, None] * cotangent.astype(jnp.float32)).astype(jnp.bfloat16)
    back = lax.dot_general(
        scaled, down_mat, (((1,), (1,)), ((), ())), preferred_element_type=jnp.float32
    )
    gate_back = (back * up * sig * (1.0 + gate * (1.0 - sig))).astype(jnp.bfloat16)
    up_back = (back * act).astype(jnp.bfloat16)
    both_back = jnp.concatenate([gate_back, up_back], axis=1)
    both_mat = jnp.concatenate([gate_mat, up_mat], axis=1)
    partial_value = lax.dot_general(
        both_back, both_mat, (((1,), (1,)), ((), ())), preferred_element_type=jnp.float32
    ).astype(jnp.bfloat16)
    returned = lax.all_to_all(
        partial_value.reshape(owners, CAP, width), "expert", split_axis=0, concat_axis=0, tiled=True
    )
    returned = returned.reshape(experts, 2, CAP, width)
    total = lax.dot_general(
        picker,
        returned[:, 0].reshape(slot_count, width),
        (((0,), (0,)), ((), ())),
        preferred_element_type=jnp.float32,
    )
    total = total + lax.dot_general(
        picker,
        returned[:, 1].reshape(slot_count, width),
        (((0,), (0,)), ((), ())),
        preferred_element_type=jnp.float32,
    )
    x_grad = total.astype(jnp.bfloat16)
    wide_grad = lax.psum_scatter(
        lax.dot_general(
            inputs, both_back, (((0,), (0,)), ((), ())), preferred_element_type=jnp.float32
        )
        .astype(jnp.bfloat16)
        .astype(jnp.bfloat16),
        "replica",
        scatter_dimension=0,
        tiled=True,
    ).astype(jnp.float32)
    half_units = gate_mat.shape[1]
    gate_grad = wide_grad[:, :half_units].astype(jnp.bfloat16)[None]
    up_grad = wide_grad[:, half_units:].astype(jnp.bfloat16)[None]
    down_local = lax.dot_general(
        hidden, scaled, (((0,), (0,)), ((), ())), preferred_element_type=jnp.float32
    )
    down_grad = lax.psum(down_local.astype(jnp.bfloat16), "replica")[None]
    return (x_grad, gate_grad, up_grad, down_grad)


def solution(mesh):
    return jax.shard_map(
        shards,
        mesh=mesh,
        in_specs=(
            P(("expert", "replica"), None),
            P(("expert", "replica"), None),
            P(("expert", "replica"), None),
            P(("expert", "replica"), None),
            P(),
            P("expert", "replica", None),
            P("expert", "replica", None),
            P("expert", None, "replica"),
        ),
        out_specs=(
            P(("expert", "replica"), None),
            P("expert", "replica", None),
            P("expert", "replica", None),
            P("expert", None, None),
        ),
        check_vma=False,
    )
```

profile of v0, /device:TPU:0, one launch (start us, length us, event | category | flops | bytes accessed | tf_op | source)
XLA Modules:
  0.0 171.9 jit_solution(11029008983379027724)
XLA Ops:
  7.2 0.0 all-gather.6.cloned.1.call-start
  7.2 0.7 all-gather.6.cloned.1.call-update
  7.9 0.0 all-gather.4.cloned.1.call-start
  7.9 0.7 all-gather.4.cloned.1.call-update
  8.6 0.0 all-gather.8.cloned.1.call-start
  8.7 0.7 all-gather.8.cloned.1.call-update
  9.4 0.7 convert_reduce_fusion.1
  10.1 0.1 copy.27
  10.2 0.2 reduce_window_sum.11
  10.4 0.1 copy.28
  10.4 0.7 convert_element_type.61
  11.1 0.8 select_reduce_fusion.2
  11.9 0.7 compare_select_fusion
  12.6 0.1 select_reduce_fusion
  12.7 0.1 convert_element_type.63
  12.8 0.1 copy.29
  12.9 0.1 broadcast_in_dim.45
  12.9 0.1 all_to_all.12
  13.0 0.7 copy.30
  13.7 7.3 %all-to-all-start = ((bf16[8,1,2]{2,1,0:T(2,128)(2,1)}), bf16[8,1,2]{2,1,0:T(2,128)(2,1)S(1)}, u32[]{:S(2)}, u32[]{:S(2)}) async-start(bf16[8,1,2]{2,1,0:T(2,128)(2,1)} %copy.30), calls=%async_computation | async-start | bytes 8192 | tf_op jit(solution)/shard_map/all_to_all | solution.py:36
  21.0 1.4 convolution_convert_fusion
  22.5 0.1 broadcast_in_dim.46
  22.6 4.9 %all-to-all-done = bf16[8,1,2]{2,1,0:T(2,128)(2,1)S(1)} async-done(((bf16[8,1,2]{2,1,0:T(2,128)(2,1)}), bf16[8,1,2]{2,1,0:T(2,128)(2,1)S(1)}, u32[]{:S(2)}, u32[]{:S(2)}) %all-to-all-start) | async-done | bytes 64 | tf_op jit(solution)/shard_map/all_to_all | solution.py:36
  27.5 0.7 broadcast_in_dim.47
  28.2 3.4 %all-to-all-start.1 = ((bf16[8,2,4096]{2,1,0:T(2,128)(2,1)}), bf16[8,2,4096]{2,1,0:T(2,128)(2,1)S(1)}, u32[]{:S(2)}, u32[]{:S(2)}) async-start(bf16[8,2,4096]{2,1,0:T(2,128)(2,1)} %bitcast), calls=%async_computation.1 | async-start | bytes 262144 | tf_op jit(solution)/shard_map/all_to_all | solution.py:35
  31.6 0.0 reduce-scatter.2.cloned.1.call-start
  31.6 0.1 reshape.51
  31.7 7.1 %all-to-all-done.1 = bf16[8,2,4096]{2,1,0:T(2,128)(2,1)S(1)} async-done(((bf16[8,2,4096]{2,1,0:T(2,128)(2,1)}), bf16[8,2,4096]{2,1,0:T(2,128)(2,1)S(1)}, u32[]{:S(2)}, u32[]{:S(2)}) %all-to-all-start.1) | async-done | bytes 131104 | tf_op jit(solution)/shard_map/all_to_all | solution.py:35
  38.8 0.1 reshape.48
  38.9 1.8 %fusion.17 = f32[16,384]{1,0:T(8,128)S(1)} fusion(bf16[16,4096]{1,0:T(8,128)(2,1)S(1)} %reshape.48, bf16[1,2048,384]{2,1,0:T(8,128)(2,1)} %all-gather.6.cloned.1.call-done), kind=kOutput, calls=%fused_computation.22 | convolution fusion | flops 25165824 | bytes 1662976 | tf_op jit(solution)/shard_map/dot_general | solution.py:52
  40.7 12.4 %all-gather.4.cloned.1.call-done = bf16[1,384,2048]{2,1,0:T(8,128)(2,1)} async-done(((bf16[1,384,512]{2,1,0:T(8,128)(2,1)}), bf16[1,384,2048]{2,1,0:T(8,128)(2,1)}) %all-gather.4.cloned.1.call-update) | async-done | bytes 1572880 | tf_op jit(solution)/shard_map/all_gather | solution.py:41
  53.1 1.9 %fusion.9 = f32[16,384]{1,0:T(8,128)S(1)} fusion(bf16[1,384,2048]{2,1,0:T(8,128)(2,1)} %all-gather.4.cloned.1.call-done, bf16[16,4096]{1,0:T(8,128)(2,1)S(1)} %reshape.48, f32[16]{0:T(128)S(1)} %reshape.51), kind=kOutput, calls=%fused_computation.11 | convolution fusion | flops 25264128 | bytes 1663488 | tf_op jit(solution)/shard_map/dot_general | solution.py:57
  55.1 19.3 %all-gather.8.cloned.1.call-done = bf16[1,2048,384]{2,1,0:T(8,128)(2,1)} async-done(((bf16[1,512,384]{2,1,0:T(8,128)(2,1)}), bf16[1,2048,384]{2,1,0:T(8,128)(2,1)}) %all-gather.8.cloned.1.call-update) | async-done | bytes 1572880 | tf_op jit(solution)/shard_map/all_gather | solution.py:39
  74.4 1.7 %multiply_convert_fusion.3 = (bf16[16,384]{1,0:T(8,128)(2,1)S(1)}, bf16[16,384]{1,0:T(8,128)(2,1)S(1)}, f32[16,384]{1,0:T(8,128)S(1)}) fusion(f32[16,384]{1,0:T(8,128)S(1)} %fusion.9, f32[16,384]{1,0:T(8,128)S(1)} %fusion.17, bf16[1,2048,384]{2,1,0:T(8,128)(2,1)} %all-gather.8.cloned.1.call-done, bf16[16,4096]{1,0:T(8,128)(2,1)S(1)} %reshape.48), kind=kOutput, calls=%fused_computation.27 | convolution fusion | flops 25245696 | bytes 1736704 | tf_op jit(solution)/shard_map/dot_general | solution.py:51
  76.1 2.7 %convolution_convert_fusion.1 = bf16[2048,768]{1,0:T(8,128)(2,1)} fusion(bf16[16,4096]{1,0:T(8,128)(2,1)S(1)} %reshape.48, bf16[16,384]{1,0:T(8,128)(2,1)S(1)} %get-tuple-element.11, bf16[16,384]{1,0:T(8,128)(2,1)S(1)} %get-tuple-element.10), kind=kOutput, calls=%fused_computation.1 | convolution fusion | flops 51953664 | bytes 3235840 | tf_op jit(solution)/shard_map/dot_general | solution.py:85
  78.8 1.4 copy-done
  80.2 0.5 copy-done.1
  80.7 0.9 fusion.6
  81.6 0.7 reshape.49
  82.3 5.5 %all-to-all-start.2 = ((bf16[8,2,2048]{2,1,0:T(2,128)(2,1)}), bf16[8,2,2048]{2,1,0:T(2,128)(2,1)S(1)}, u32[]{:S(2)}, u32[]{:S(2)}) async-start(bf16[8,2,2048]{2,1,0:T(2,128)(2,1)} %reshape.49), calls=%async_computation.2 | async-start | bytes 131072 | tf_op jit(solution)/shard_map/all_to_all | solution.py:67
  87.9 1.8 %fusion.4 = bf16[1,384,2048]{2,1,0:T(8,128)(2,1)} fusion(bf16[16,4096]{1,0:T(8,128)(2,1)S(1)} %reshape.48, f32[16]{0:T(128)S(1)} %reshape.51, f32[16,384]{1,0:T(8,128)S(1)} %fusion.17, f32[16,384]{1,0:T(8,128)S(1)} %get-tuple-element.12), kind=kOutput, calls=%fused_computation.7 | convolution fusion | flops 26087424 | bytes 1688064 | tf_op jit(solution)/shard_map/dot_general | solution.py:97
  89.7 5.1 %all-to-all-done.2 = bf16[8,2,2048]{2,1,0:T(2,128)(2,1)S(1)} async-done(((bf16[8,2,2048]{2,1,0:T(2,128)(2,1)}), bf16[8,2,2048]{2,1,0:T(2,128)(2,1)S(1)}, u32[]{:S(2)}, u32[]{:S(2)}) %all-to-all-start.2) | async-done | bytes 65568 | tf_op jit(solution)/shard_map/all_to_all | solution.py:67
  94.8 0.3 fusion.29
  95.2 1.1 fusion.5
  96.3 20.6 %reduce-scatter.2.cloned.1.call-done = bf16[512,768]{1,0:T(8,128)(2,1)} async-done(((bf16[2048,768]{1,0:T(8,128)(2,1)}), bf16[512,768]{1,0:T(8,128)(2,1)}) %reduce-scatter.2.cloned.1.call-update) | async-done | bytes 786448 | tf_op jit(solution)/shard_map/reduce_scatter | solution.py:84
  116.9 2.1 %slice_bitcast_fusion = (bf16[1,512,384]{2,1,0:T(8,128)(2,1)}, bf16[1,512,384]{2,1,0:T(8,128)(2,1)}) fusion(bf16[512,768]{1,0:T(8,128)(2,1)} %reduce-scatter.2.cloned.1.call-done), kind=kLoop, calls=%fused_computation.16 | loop fusion | bytes 1572864 | tf_op jit(solution)/shard_map/broadcast_in_dim | solution.py:96
  119.0 43.6 %all-reduce.2.cloned.1.call-done = bf16[1,384,2048]{2,1,0:T(8,128)(2,1)} async-done(((bf16[1,384,2048]{2,1,0:T(8,128)(2,1)}), bf16[1,384,2048]{2,1,0:T(8,128)(2,1)}) %all-reduce.2.cloned.1.call-update) | async-done | bytes 1572880 | tf_op jit(solution)/shard_map/psum | solution.py:100
  162.6 2.7 %copy.32 = bf16[1,384,2048]{2,1,0:T(8,128)(2,1)} copy(bf16[1,384,2048]{2,1,0:T(8,128)(2,1)} %all-reduce.2.cloned.1.call-done) | data formatting | bytes 3145728
  (11 shorter events, 0.2 us)
Async XLA Ops:
  7.2 31.8 %all-gather.6.cloned.1.call-start = ((), (), s32[]{:S(2)}) async-start(), calls=%async_computation.5 | async-start | bytes 1966080 | tf_op jit(solution)/shard_map/all_gather | solution.py:40
  7.9 45.2 %all-gather.4.cloned.1.call-start = ((), (), s32[]{:S(2)}) async-start(), calls=%async_computation.4 | async-start | bytes 1966080 | tf_op jit(solution)/shard_map/all_gather | solution.py:41
  8.6 65.7 %all-gather.8.cloned.1.call-start = ((), (), s32[]{:S(2)}) async-start(), calls=%async_computation.6 | async-start | bytes 1966080 | tf_op jit(solution)/shard_map/all_gather | solution.py:39
  13.7 13.7 %all-to-all-start = ((bf16[8,1,2]{2,1,0:T(2,128)(2,1)}), bf16[8,1,2]{2,1,0:T(2,128)(2,1)S(1)}, u32[]{:S(2)}, u32[]{:S(2)}) async-start(bf16[8,1,2]{2,1,0:T(2,128)(2,1)} %copy.30), calls=%async_computation | async-start | bytes 8192 | tf_op jit(solution)/shard_map/all_to_all | solution.py:36
  28.2 10.7 %all-to-all-start.1 = ((bf16[8,2,4096]{2,1,0:T(2,128)(2,1)}), bf16[8,2,4096]{2,1,0:T(2,128)(2,1)S(1)}, u32[]{:S(2)}, u32[]{:S(2)}) async-start(bf16[8,2,4096]{2,1,0:T(2,128)(2,1)} %bitcast), calls=%async_computation.1 | async-start | bytes 262144 | tf_op jit(solution)/shard_map/all_to_all | solution.py:35
  31.6 85.4 %reduce-scatter.2.cloned.1.call-start = ((), (), s32[]{:S(2)}) async-start(), calls=%async_computation.7 | async-start | bytes 3932160 | tf_op jit(solution)/shard_map/reduce_scatter | solution.py:84
  78.8 1.4 copy-start
  78.8 1.9 %copy-start.1 = (bf16[1,2048,384]{2,1,0:T(8,128)(2,1)S(1)}, bf16[1,2048,384]{2,1,0:T(8,128)(2,1)}, u32[]{:S(2)}) copy-start(bf16[1,2048,384]{2,1,0:T(8,128)(2,1)} %all-gather.8.cloned.1.call-done) | copy-start | bytes 4718596
  82.3 12.4 %all-to-all-start.2 = ((bf16[8,2,2048]{2,1,0:T(2,128)(2,1)}), bf16[8,2,2048]{2,1,0:T(2,128)(2,1)S(1)}, u32[]{:S(2)}, u32[]{:S(2)}) async-start(bf16[8,2,2048]{2,1,0:T(2,128)(2,1)} %reshape.49), calls=%async_computation.2 | async-start | bytes 131072 | tf_op jit(solution)/shard_map/all_to_all | solution.py:67
  87.8 74.8 %all-reduce.2.cloned.1.call-start = ((), (), s32[]{:S(2)}) async-start(), calls=%async_computation.8 | async-start | bytes 3145728 | tf_op jit(solution)/shard_map/psum | solution.py:100
Sparse Core Ops, SparseCore 0:
  9.5 22.3 all-gather.5
  33.5 19.6 all-gather.3
  54.7 19.6 all-gather.7
  79.0 37.9 reduce-scatter.1
  119.7 42.8 all-reduce.1
where the time goes:
time: 172 us
  waiting for transfers between devices  115 us (67%)
  starting transfers between devices  16.4 us (10%)
  between operations  13.9 us (8%)
  matrix products  13.7 us (8%)
  local copies, waits for them, and re-layouts  9.59 us (6%)
  other arithmetic  3.13 us (2%)
    psum x1, waiting for transfers between devices, shards(): down_grad = lax.psum(down_local.astype(jnp.bfloat16), 'replica')[None]  43.6 us
    reduce_scatter x1, waiting for transfers between devices, shards(): lax.psum_scatter(lax.dot_general(inputs, both_back, (((0,), (0,)), ((), (...  20.6 us
    all_gather x1, waiting for transfers between devices, shards(): lax.all_gather(w_gate, 'replica', axis=1, tiled=True)  19.3 us
    all_gather x1, waiting for transfers between devices, shards(): lax.all_gather(w_down, 'replica', axis=2, tiled=True)  12.4 us
    all_to_all x1, starting transfers between devices, shards(): lax.all_to_all(send_weight, 'expert', split_axis=0, concat_axis=0, tiled=...  7.31 us
    all_to_all x1, waiting for transfers between devices, shards(): lax.all_to_all(send_rows, 'expert', split_axis=0, concat_axis=0, tiled=True)  7.13 us
    all_to_all x1, starting transfers between devices, shards(): lax.all_to_all(partial_value.reshape(owners, CAP, width), 'expert', split...  5.52 us
    all_to_all x1, waiting for transfers between devices, shards(): lax.all_to_all(partial_value.reshape(owners, CAP, width), 'expert', split...  5.08 us
  transfers between devices with their start and end apart: 8, of which 7 were waited for; matrix products, arithmetic and copies ran while one was open for 10% of the time, Pallas kernels for 0%

commit v1 on v0

--- a/solution.py
+++ b/solution.py
@@ -36,7 +36,9 @@
         lax.all_to_all(send_weight, "expert", split_axis=0, concat_axis=0, tiled=True),
     )
     gate_all, up_all, down_all = (
-        lax.all_gather(w_gate, "replica", axis=1, tiled=True),
+        jnp.concatenate(
+            lax.all_to_all(jnp.stack([w_gate] * lax.axis_size("replica")), "replica", 0, 0), axis=1
+        ),
         lax.all_gather(w_up, "replica", axis=1, tiled=True),
         lax.all_gather(w_down, "replica", axis=2, tiled=True),
     )

time: 172 us -> 163 us (0.948)
  waiting for transfers between devices: 115 us -> 99.3 us
  blocking collectives: 0 us -> 9.74 us
    all_gather x1 -> x0, waiting for transfers between devices: 19.3 us -> none  [shards(): lax.all_gather(w_gate, 'replica', axis=1, tiled=True)]
    all_to_all x0 -> x1, blocking collectives: none -> 9.74 us  [shards(): lax.all_to_all(send_rows, 'expert', split_axis=0, concat_axis=0, tiled=True)]
    all_gather x1, waiting for transfers between devices: 12.4 us -> 17 us  [shards(): lax.all_gather(w_down, 'replica', axis=2, tiled=True)]
    all_to_all x1, starting transfers between devices: 5.52 us -> 3.69 us  [shards(): lax.all_to_all(partial_value.reshape(owners, CAP, width), 'expert', split...]
  transfers between devices with their start and end apart: 8 -> 7, of which waited for: 7 -> 6; matrix products, arithmetic and copies ran while one was open for 10% -> 11% of each run, Pallas kernels for 0% -> 0%
where the time goes in v1:
time: 163 us
  waiting for transfers between devices  99.3 us (61%)
  starting transfers between devices  14.7 us (9%)
  between operations  13.9 us (9%)
  matrix products  12.3 us (8%)
  local copies, waits for them, and re-layouts  9.75 us (6%)
  blocking collectives  9.74 us (6%)
  other arithmetic  3.13 us (2%)
    psum x1, waiting for transfers between devices, shards(): down_grad = lax.psum(down_local.astype(jnp.bfloat16), 'replica')[None]  43.6 us
    reduce_scatter x1, waiting for transfers between devices, shards(): lax.psum_scatter(lax.dot_general(inputs, both_back, (((0,), (0,)), ((), (...  21 us
    all_gather x1, waiting for transfers between devices, shards(): lax.all_gather(w_down, 'replica', axis=2, tiled=True)  17 us
    all_to_all x1, blocking collectives, shards(): lax.all_to_all(send_rows, 'expert', split_axis=0, concat_axis=0, tiled=True)  9.74 us
    all_to_all x1, starting transfers between devices, shards(): lax.all_to_all(send_weight, 'expert', split_axis=0, concat_axis=0, tiled=...  7.31 us
    all_to_all x1, waiting for transfers between devices, shards(): lax.all_to_all(jnp.stack([w_gate] * lax.axis_size('replica')), 'replica',...  6.2 us
    all_to_all x1, waiting for transfers between devices, shards(): lax.all_to_all(partial_value.reshape(owners, CAP, width), 'expert', split...  5.08 us
    all_to_all x1, waiting for transfers between devices, shards(): lax.all_to_all(send_weight, 'expert', split_axis=0, concat_axis=0, tiled=...  4.89 us
  transfers between devices with their start and end apart: 7, of which 6 were waited for; matrix products, arithmetic and copies ran while one was open for 11% of the time, Pallas kernels for 0%

profile of v1, /device:TPU:0, one launch (start us, length us, event | category | flops | bytes accessed | tf_op | source)
XLA Modules:
  0.0 162.7 jit_solution(8269352875426419456)
XLA Ops:
  7.2 0.0 all-gather.5.cloned.1.call-start
  7.2 0.7 all-gather.5.cloned.1.call-update
  7.9 0.0 all-gather.3.cloned.1.call-start
  8.0 0.7 all-gather.3.cloned.1.call-update
  8.7 0.7 convert_reduce_fusion.1
  9.4 0.1 copy.27
  9.5 0.2 reduce_window_sum.11
  9.6 0.1 copy.28
  9.7 0.7 convert_element_type.61
  10.4 0.8 select_reduce_fusion.2
  11.1 0.7 compare_select_fusion
  11.8 0.1 select_reduce_fusion
  11.9 0.1 convert_element_type.63
  12.0 0.1 copy.29
  12.1 0.1 broadcast_in_dim.45
  12.2 0.1 all_to_all.15
  12.3 0.7 copy.30
  13.0 7.3 %all-to-all-start = ((bf16[8,1,2]{2,1,0:T(2,128)(2,1)}), bf16[8,1,2]{2,1,0:T(2,128)(2,1)S(1)}, u32[]{:S(2)}, u32[]{:S(2)}) async-start(bf16[8,1,2]{2,1,0:T(2,128)(2,1)} %copy.30), calls=%async_computation | async-start | bytes 8192 | tf_op jit(solution)/shard_map/all_to_all | solution.py:36
  20.3 1.4 convolution_convert_fusion
  21.8 0.1 broadcast_in_dim.46
  21.8 4.9 %all-to-all-done = bf16[8,1,2]{2,1,0:T(2,128)(2,1)S(1)} async-done(((bf16[8,1,2]{2,1,0:T(2,128)(2,1)}), bf16[8,1,2]{2,1,0:T(2,128)(2,1)S(1)}, u32[]{:S(2)}, u32[]{:S(2)}) %all-to-all-start) | async-done | bytes 64 | tf_op jit(solution)/shard_map/all_to_all | solution.py:36
  26.7 0.1 broadcast_in_dim.47
  26.8 9.7 %all_to_all.24 = bf16[8,2,4096]{2,1,0:T(2,128)(2,1)S(1)} all-to-all(bf16[8,2,4096]{2,1,0:T(2,128)(2,1)S(1)} %bitcast.27), channel_id=1, replica_groups=mesh['expert'=8,'replica'=4] {'expert'}, dimensions={0} | all-to-all | bytes 262144 | tf_op jit(solution)/shard_map/all_to_all | solution.py:35
  36.5 1.3 stack.2
  37.8 3.6 %all-to-all-start.2 = ((bf16[4,1,512,384]{3,2,1,0:T(8,128)(2,1)}), bf16[4,1,512,384]{3,2,1,0:T(8,128)(2,1)S(1)}, u32[]{:S(2)}, u32[]{:S(2)}) async-start(bf16[4,1,512,384]{3,2,1,0:T(8,128)(2,1)} %stack.2), calls=%async_computation.2 | async-start | bytes 3145728 | tf_op jit(solution)/shard_map/all_to_all | solution.py:40
  41.4 0.0 reduce-scatter.2.cloned.1.call-start
  41.5 0.1 reshape.54
  41.6 0.1 reshape.51
  41.6 0.0 all-gather.5.cloned.1.call-done
  41.7 1.7 %fusion.17 = f32[16,384]{1,0:T(8,128)S(1)} fusion(bf16[16,4096]{1,0:T(8,128)(2,1)S(1)} %reshape.51, bf16[1,2048,384]{2,1,0:T(8,128)(2,1)} %all-gather.5.cloned.1.call-done), kind=kOutput, calls=%fused_computation.22 | convolution fusion | flops 25165824 | bytes 1662976 | tf_op jit(solution)/shard_map/dot_general | solution.py:54
  43.4 17.0 %all-gather.3.cloned.1.call-done = bf16[1,384,2048]{2,1,0:T(8,128)(2,1)} async-done(((bf16[1,384,512]{2,1,0:T(8,128)(2,1)}), bf16[1,384,2048]{2,1,0:T(8,128)(2,1)}) %all-gather.3.cloned.1.call-update) | async-done | bytes 1572880 | tf_op jit(solution)/shard_map/all_gather | solution.py:43
  60.4 1.9 %fusion.9 = f32[16,384]{1,0:T(8,128)S(1)} fusion(bf16[1,384,2048]{2,1,0:T(8,128)(2,1)} %all-gather.3.cloned.1.call-done, bf16[16,4096]{1,0:T(8,128)(2,1)S(1)} %reshape.51, f32[16]{0:T(128)S(1)} %reshape.54), kind=kOutput, calls=%fused_computation.11 | convolution fusion | flops 25264128 | bytes 1663488 | tf_op jit(solution)/shard_map/dot_general | solution.py:59
  62.3 6.2 %all-to-all-done.2 = bf16[4,1,512,384]{3,2,1,0:T(8,128)(2,1)S(1)} async-done(((bf16[4,1,512,384]{3,2,1,0:T(8,128)(2,1)}), bf16[4,1,512,384]{3,2,1,0:T(8,128)(2,1)S(1)}, u32[]{:S(2)}, u32[]{:S(2)}) %all-to-all-start.2) | async-done | bytes 1572896 | tf_op jit(solution)/shard_map/all_to_all | solution.py:40
  68.5 0.3 multiply_convert_fusion.3
  68.8 2.7 %convolution_convert_fusion.1 = bf16[2048,768]{1,0:T(8,128)(2,1)} fusion(bf16[16,4096]{1,0:T(8,128)(2,1)S(1)} %reshape.51, bf16[16,384]{1,0:T(8,128)(2,1)S(1)} %get-tuple-element.11, bf16[16,384]{1,0:T(8,128)(2,1)S(1)} %get-tuple-element.10), kind=kOutput, calls=%fused_computation.1 | convolution fusion | flops 51953664 | bytes 3235840 | tf_op jit(solution)/shard_map/dot_general | solution.py:87
  71.6 1.4 copy-done
  73.0 0.9 fusion.6
  73.9 0.7 reshape.52
  74.6 3.7 %all-to-all-start.3 = ((bf16[8,2,2048]{2,1,0:T(2,128)(2,1)}), bf16[8,2,2048]{2,1,0:T(2,128)(2,1)S(1)}, u32[]{:S(2)}, u32[]{:S(2)}) async-start(bf16[8,2,2048]{2,1,0:T(2,128)(2,1)} %reshape.52), calls=%async_computation.3 | async-start | bytes 131072 | tf_op jit(solution)/shard_map/all_to_all | solution.py:69
  78.3 0.0 all-reduce.2.cloned.1.call-start
  78.3 1.8 %fusion.4 = bf16[1,384,2048]{2,1,0:T(8,128)(2,1)} fusion(bf16[16,4096]{1,0:T(8,128)(2,1)S(1)} %reshape.51, f32[16]{0:T(128)S(1)} %reshape.54, f32[16,384]{1,0:T(8,128)S(1)} %fusion.17, f32[16,384]{1,0:T(8,128)S(1)} %get-tuple-element.12), kind=kOutput, calls=%fused_computation.7 | convolution fusion | flops 26087424 | bytes 1688064 | tf_op jit(solution)/shard_map/dot_general | solution.py:99
  80.1 5.1 %all-to-all-done.3 = bf16[8,2,2048]{2,1,0:T(2,128)(2,1)S(1)} async-done(((bf16[8,2,2048]{2,1,0:T(2,128)(2,1)}), bf16[8,2,2048]{2,1,0:T(2,128)(2,1)S(1)}, u32[]{:S(2)}, u32[]{:S(2)}) %all-to-all-start.3) | async-done | bytes 65568 | tf_op jit(solution)/shard_map/all_to_all | solution.py:69
  85.3 0.3 fusion.28
  85.6 1.1 fusion.5
  86.8 21.0 %reduce-scatter.2.cloned.1.call-done = bf16[512,768]{1,0:T(8,128)(2,1)} async-done(((bf16[2048,768]{1,0:T(8,128)(2,1)}), bf16[512,768]{1,0:T(8,128)(2,1)}) %reduce-scatter.2.cloned.1.call-update) | async-done | bytes 786448 | tf_op jit(solution)/shard_map/reduce_scatter | solution.py:86
  107.8 2.1 %slice_bitcast_fusion = (bf16[1,512,384]{2,1,0:T(8,128)(2,1)}, bf16[1,512,384]{2,1,0:T(8,128)(2,1)}) fusion(bf16[512,768]{1,0:T(8,128)(2,1)} %reduce-scatter.2.cloned.1.call-done), kind=kLoop, calls=%fused_computation.16 | loop fusion | bytes 1572864 | tf_op jit(solution)/shard_map/broadcast_in_dim | solution.py:98
  109.8 43.6 %all-reduce.2.cloned.1.call-done = bf16[1,384,2048]{2,1,0:T(8,128)(2,1)} async-done(((bf16[1,384,2048]{2,1,0:T(8,128)(2,1)}), bf16[1,384,2048]{2,1,0:T(8,128)(2,1)}) %all-reduce.2.cloned.1.call-update) | async-done | bytes 1572880 | tf_op jit(solution)/shard_map/psum | solution.py:102
  153.5 2.7 %copy.32 = bf16[1,384,2048]{2,1,0:T(8,128)(2,1)} copy(bf16[1,384,2048]{2,1,0:T(8,128)(2,1)} %all-reduce.2.cloned.1.call-done) | data formatting | bytes 3145728
  (10 shorter events, 0.1 us)
Async XLA Ops:
  7.2 29.4 %copy-start.1 = (bf16[1,512,384]{2,1,0:T(8,128)(2,1)S(1)}, bf16[1,512,384]{2,1,0:T(8,128)(2,1)}, u32[]{:S(2)}) copy-start(bf16[1,512,384]{2,1,0:T(8,128)(2,1)} %param.13) | copy-start | bytes 1179652
  7.2 34.5 %all-gather.5.cloned.1.call-start = ((), (), s32[]{:S(2)}) async-start(), calls=%async_computation.6 | async-start | bytes 1966080 | tf_op jit(solution)/shard_map/all_gather | solution.py:42
  7.9 52.5 %all-gather.3.cloned.1.call-start = ((), (), s32[]{:S(2)}) async-start(), calls=%async_computation.5 | async-start | bytes 1966080 | tf_op jit(solution)/shard_map/all_gather | solution.py:43
  13.0 13.7 %all-to-all-start = ((bf16[8,1,2]{2,1,0:T(2,128)(2,1)}), bf16[8,1,2]{2,1,0:T(2,128)(2,1)S(1)}, u32[]{:S(2)}, u32[]{:S(2)}) async-start(bf16[8,1,2]{2,1,0:T(2,128)(2,1)} %copy.30), calls=%async_computation | async-start | bytes 8192 | tf_op jit(solution)/shard_map/all_to_all | solution.py:36
  37.8 30.7 %all-to-all-start.2 = ((bf16[4,1,512,384]{3,2,1,0:T(8,128)(2,1)}), bf16[4,1,512,384]{3,2,1,0:T(8,128)(2,1)S(1)}, u32[]{:S(2)}, u32[]{:S(2)}) async-start(bf16[4,1,512,384]{3,2,1,0:T(8,128)(2,1)} %stack.2), calls=%async_computation.2 | async-start | bytes 3145728 | tf_op jit(solution)/shard_map/all_to_all | solution.py:40
  41.4 66.3 %reduce-scatter.2.cloned.1.call-start = ((), (), s32[]{:S(2)}) async-start(), calls=%async_computation.7 | async-start | bytes 3932160 | tf_op jit(solution)/shard_map/reduce_scatter | solution.py:86
  71.5 1.4 copy-start
  74.6 10.6 %all-to-all-start.3 = ((bf16[8,2,2048]{2,1,0:T(2,128)(2,1)}), bf16[8,2,2048]{2,1,0:T(2,128)(2,1)S(1)}, u32[]{:S(2)}, u32[]{:S(2)}) async-start(bf16[8,2,2048]{2,1,0:T(2,128)(2,1)} %reshape.52), calls=%async_computation.3 | async-start | bytes 131072 | tf_op jit(solution)/shard_map/all_to_all | solution.py:69
  78.3 75.2 %all-reduce.2.cloned.1.call-start = ((), (), s32[]{:S(2)}) async-start(), calls=%async_computation.8 | async-start | bytes 3145728 | tf_op jit(solution)/shard_map/psum | solution.py:102
Sparse Core Ops, SparseCore 0:
  9.5 22.3 all-gather.4
  33.5 26.8 all-gather.2
  71.7 36.0 reduce-scatter.1
  110.6 42.8 all-reduce.1
